TPU v7x, 32 devices: a whole 2x2x4 slice. The times are simulated.
32 devices in a mesh: seg: 4 (over y, core), sub: 8 (over z, x).
Axes of the slice: x: 2, y: 2, z: 4, core: 2. Of those that a mesh axis runs over, the one named last changes fastest.
Arguments:
- nodal_loads: float32 [4, 8, 32, 3072], P('seg', 'sub'), may hold values from -6 to 6
- schur_matrix: bfloat16 [4, 8, 3072, 3072], P('seg', 'sub'), may hold values from -2 to 9, as said below
- face_rows: int32 [4, 8, 3072], P('seg', 'sub'), may hold values from 0 to 3071, each once within a row
- face_len: int32 [4, 8, 2], replicated, may hold values from 192 to 768, as said below
- relax_step: float32 [4, 8], P('seg', 'sub'), may hold values from 0.03 to 0.1
- coarse_basis: float32 [4, 8, 4, 3072], P('seg', 'sub'), may hold values from -0.625 to 0.625
- primal_index: int32 [4, 8, 4], replicated, may hold values from 0 to 71, as said below
- coarse_inverse: float32 [72, 72], replicated, may hold values from -1 to 1.5, as said below
Outputs:
- solution: float32 [4, 8, 32, 3072], P('seg', 'sub')
- residual: float32 [4, 8, 32, 3072], P('seg', 'sub')
Inputs may be any that keep to these rules, and one draw needn't show every extreme that they name: `schur_matrix`: symmetric in its last two dimensions and positive definite for each subdomain. `face_len`: entry [s, j, 0] counts the shared slots of the face between subdomains j and (j+1) mod 8 of segment s; entry [s, j, 1] those of the face between segments s and s+1 at subdomain j (not read for the last segment). Some entry [s, j, 0] equals 768. `primal_index`: one global number for each face: the face between subdomains j and (j+1) mod 8 of segment s, and the face below segment s at subdomain j (and above the last segment), numbered in a random order. Subdomains sharing a face name the same number; a face at the bridge's ends belongs to one subdomain only. `coarse_inverse`: symmetric positive definite.
All inputs are finite; a program needn't handle non-finite values.
Results may differ from a plain program's by a relative error of at most 0.0015.
Values sent between devices are 32-bit elements; how exact they have to be, the bound alone decides.
A program may use at most 128 MiB of HBM per device.

v0:
```python
import jax
import jax.numpy as jnp
from jax import lax
from jax.sharding import PartitionSpec as P

DEG = 3
ITERS = 3


HIGH = lax.Precision.HIGHEST


def with_halo(cells, sides, width, closed):
    for axis, dim in sides:
        count = lax.axis_size(axis)
        ends = count if closed else count - 1
        head = lax.slice_in_dim(cells, 0, width, axis=dim)
        tail = lax.slice_in_dim(cells, cells.shape[dim] - width, cells.shape[dim], axis=dim)
        cells = jnp.concatenate(
            [
                lax.ppermute(tail, axis, [(i, (i + 1) % count) for i in range(ends)]),
                cells,
                lax.ppermute(head, axis, [((i + 1) % count, i) for i in range(ends)]),
            ],
            axis=dim,
        )
    return cells


def symmetric(matrix):
    return 0.5 * (matrix + matrix.T)


def body(
    nodal_loads,
    schur_matrix,
    face_rows,
    face_len,
    relax_step,
    coarse_basis,
    primal_index,
    coarse_inverse,
):
    seg_at = lax.axis_index("seg")
    sub_at = lax.axis_index("sub")
    seg_count = lax.axis_size("seg")
    sub_count = lax.axis_size("sub")
    loads = nodal_loads[0, 0]
    matrix = schur_matrix[0, 0]
    slot_rows = face_rows[0, 0]
    relax = relax_step[0, 0]
    basis = coarse_basis[0, 0]
    width = matrix.shape[0]
    face_width = width // 4
    block = loads.shape[0]
    coarse_count = coarse_inverse.shape[0]
    lengths = jnp.stack(
        [
            face_len[seg_at, (sub_at + sub_count - 1) % sub_count, 0],
            face_len[seg_at, sub_at, 0],
            jnp.where(seg_at > 0, face_len[jnp.maximum(seg_at - 1, 0), sub_at, 1], 0),
            jnp.where(seg_at < seg_count - 1, face_len[seg_at, sub_at, 1], 0),
        ]
    )
    live_mask = (jnp.arange(face_width, dtype=jnp.int32)[None, :] < lengths[:, None]).astype(
        jnp.float32
    )
    live_weight = (
        jnp.zeros((width,), jnp.float32).at[slot_rows].set(1.0 - 0.5 * live_mask.reshape(-1))
    )
    my_faces = primal_index[seg_at, sub_at]
    coarse_columns = jnp.take(coarse_inverse, my_faces, axis=1)

    def assemble(values):
        slots = jnp.take(values, slot_rows, axis=1).reshape(block, 4, face_width) * live_mask[None]
        across = with_halo(slots[:, 0:2], (("sub", 1),), 1, True)
        along = with_halo(slots[:, 2:4], (("seg", 1),), 1, False)
        received = (
            jnp.stack([across[:, 0], across[:, 3], along[:, 0], along[:, 3]], axis=1)
            * live_mask[None]
        )
        return values.at[:, slot_rows].add(received.reshape(block, width))

    def local_product(values):
        upper = values.astype(jnp.bfloat16)
        upper_back = lax.optimization_barrier(upper).astype(jnp.float32)
        lower = (values - upper_back).astype(jnp.bfloat16)
        stacked = jnp.concatenate([upper, lower], axis=0)
        both = jnp.dot(stacked, matrix, preferred_element_type=jnp.float32)
        return both[:block] + both[block:]

    def global_inner(local_terms):
        return lax.psum(local_terms, ("seg", "sub"))

    def precondition(weighted):
        solve = relax * weighted
        for sweep in range(DEG):
            solve = relax * weighted + solve - relax * local_product(solve)
        local_coarse = jnp.dot(weighted, basis.T, precision=HIGH)
        table = (my_faces[:, None] == jnp.arange(coarse_count, dtype=jnp.int32)[None, :]).astype(
            jnp.float32
        )
        coarse_sum = lax.psum(jnp.dot(local_coarse, table, precision=HIGH), ("seg", "sub"))
        picked = jnp.dot(coarse_sum, coarse_columns, precision=HIGH)
        correction = jnp.dot(picked, basis, precision=HIGH)
        return assemble((solve + correction) * live_weight[None, :])

    solution = jnp.zeros_like(loads)
    partial_residual = loads
    assembled = assemble(partial_residual)
    precond = precondition(assembled * live_weight[None, :])
    direction = precond
    rho = symmetric(global_inner(jnp.dot(precond, partial_residual.T, precision=HIGH)))
    for iteration in range(ITERS):
        partial_image = local_product(direction)
        curvature = symmetric(global_inner(jnp.dot(direction, partial_image.T, precision=HIGH)))
        factor = jnp.linalg.cholesky(curvature)
        alpha = jax.scipy.linalg.cho_solve((factor, True), rho)
        solution = solution + jnp.dot(alpha.T, direction, precision=HIGH)
        partial_residual = partial_residual - jnp.dot(alpha.T, partial_image, precision=HIGH)
        assembled = assemble(partial_residual)
        if iteration + 1 < ITERS:
            precond = precondition(assembled * live_weight[None, :])
            rho_next = symmetric(global_inner(jnp.dot(precond, partial_residual.T, precision=HIGH)))
            factor_rho = jnp.linalg.cholesky(rho)
            beta = jax.scipy.linalg.cho_solve((factor_rho, True), rho_next)
            direction = precond + jnp.dot(beta.T, direction, precision=HIGH)
            rho = rho_next
    return (solution[None, None], assembled[None, None])


def solution(mesh):
    placed = (
        P("seg", "sub", None, None),
        P("seg", "sub", None, None),
        P("seg", "sub", None),
        P(),
        P("seg", "sub"),
        P("seg", "sub", None, None),
        P(),
        P(),
    )
    return jax.shard_map(
        body,
        mesh=mesh,
        in_specs=placed,
        out_specs=(P("seg", "sub", None, None), P("seg", "sub", None, None)),
        check_vma=False,
    )
```

profile of v0, /device:TPU:0, one launch (start us, length us, event | category | flops | bytes accessed | tf_op | source)
XLA Modules:
  0.0 883.9 jit_solution(13799291904758043335)
XLA Ops:
  7.8 10.9 %gather_fusion.1 = f32[3072,32]{1,0:T(8,128)} fusion(f32[32,3072]{0,1:T(8,128)S(1)} %copy.116, s32[3072]{0:T(1024)S(1)} %fusion.141), kind=kCustom, calls=%fused_computation.clone | custom fusion | bytes 798720 | tf_op jit(solution)/shard_map/jit(_take)/gather | solution.py:75
  35.0 11.8 %scatter_custom_fusion.1 = f32[3072]{0:T(1024)S(1)} fusion(s32[3072]{0:T(1024)S(1)} %bitcast.273, f32[3072]{0:T(1024)S(1)} %select_subtract_fusion, f32[]{:T(128)} %constant.98.clone.1), kind=kCustom, calls=%fused_computation.251 | custom fusion | bytes 12292 | tf_op jit(solution)/shard_map/scatter | solution.py:69
  49.1 17.5 %scatter_fusion = f32[32,3072]{0,1:T(8,128)S(1)} fusion(f32[32,3072]{0,1:T(8,128)S(1)} %copy.116, s32[3072]{0:T(1024)S(1)} %bitcast.274, f32[3072,32]{1,0:T(8,128)S(1)} %copy.117), kind=kCustom, calls=%fused_computation.8 | custom fusion | flops 98304 | bytes 1191936 | tf_op jit(solution)/shard_map/scatter-add | solution.py:82
  67.3 8.2 fusion.22
  75.7 8.7 fusion.20
  88.8 52.7 %psum.63 = f32[32,72]{1,0:T(8,128)S(1)} all-reduce(f32[32,72]{1,0:T(8,128)S(1)} %fusion.148), channel_id=1, replica_groups=mesh['seg'=4,'sub'=8] {'seg','sub'}, use_global_device_ids=true, to_apply=%region_2.4 | all-reduce | flops 2304 | bytes 18432 | tf_op jit(solution)/shard_map/psum | solution.py:103
  142.7 10.9 %gather_fusion.2 = f32[3072,32]{1,0:T(8,128)} fusion(f32[32,3072]{0,1:T(8,128)S(1)} %copy.123, s32[3072]{0:T(1024)S(1)} %fusion.141), kind=kCustom, calls=%fused_computation.1.clone | custom fusion | bytes 798720 | tf_op jit(solution)/shard_map/jit(_take)/gather | solution.py:75
  172.7 17.5 %scatter_fusion.1 = f32[32,3072]{0,1:T(8,128)S(1)} fusion(f32[32,3072]{0,1:T(8,128)S(1)} %copy.123, s32[3072]{0:T(1024)S(1)} %bitcast.275, f32[3072,32]{1,0:T(8,128)S(1)} %copy.124), kind=kCustom, calls=%fused_computation.10 | custom fusion | flops 98304 | bytes 1191936 | tf_op jit(solution)/shard_map/scatter-add | solution.py:82
  194.0 8.3 fusion.16
  205.7 39.8 %all-reduce = (f32[32,32]{1,0:T(8,128)S(1)}, f32[32,32]{1,0:T(8,128)S(1)}) all-reduce(f32[32,32]{1,0:T(8,128)S(1)} %fusion.177, f32[32,32]{1,0:T(8,128)S(1)} %fusion.95), channel_id=1, replica_groups=mesh['seg'=4,'sub'=8] {'seg','sub'}, use_global_device_ids=true, to_apply=%region_7.10 | all-reduce | flops 2048 | bytes 16384 | tf_op jit(solution)/shard_map/psum | solution.py:93
  259.7 10.9 %gather_fusion.3 = f32[3072,32]{1,0:T(8,128)} fusion(f32[32,3072]{0,1:T(8,128)S(1)} %copy.131, s32[3072]{0:T(1024)S(1)} %fusion.141), kind=kCustom, calls=%fused_computation.2.clone | custom fusion | bytes 798720 | tf_op jit(solution)/shard_map/jit(_take)/gather | solution.py:75
  292.4 18.2 %scatter_fusion.2 = f32[32,3072]{0,1:T(8,128)S(1)} fusion(f32[32,3072]{0,1:T(8,128)S(1)} %copy.131, s32[3072]{0:T(1024)S(1)} %bitcast.276, f32[3072,32]{1,0:T(8,128)} %copy.132), kind=kCustom, calls=%fused_computation.11 | custom fusion | flops 98304 | bytes 1191936 | tf_op jit(solution)/shard_map/scatter-add | solution.py:82
  315.4 8.2 fusion.14
  323.9 8.8 fusion.12
  337.5 42.8 %psum.66 = f32[32,72]{1,0:T(8,128)S(1)} all-reduce(f32[32,72]{1,0:T(8,128)S(1)} %fusion.147), channel_id=1, replica_groups=mesh['seg'=4,'sub'=8] {'seg','sub'}, use_global_device_ids=true, to_apply=%region_9.13 | all-reduce | flops 2304 | bytes 18432 | tf_op jit(solution)/shard_map/psum | solution.py:103
  384.4 10.9 %gather_fusion.4 = f32[3072,32]{1,0:T(8,128)} fusion(f32[32,3072]{0,1:T(8,128)S(1)} %copy.137, s32[3072]{0:T(1024)S(1)} %fusion.141), kind=kCustom, calls=%fused_computation.3.clone | custom fusion | bytes 798720 | tf_op jit(solution)/shard_map/jit(_take)/gather | solution.py:75
  419.6 18.0 %scatter_fusion.3 = f32[32,3072]{0,1:T(8,128)S(1)} fusion(f32[32,3072]{0,1:T(8,128)S(1)} %copy.137, s32[3072]{0:T(1024)S(1)} %bitcast.277, f32[3072,32]{1,0:T(8,128)} %copy.138), kind=kCustom, calls=%fused_computation.12 | custom fusion | flops 98304 | bytes 1191936 | tf_op jit(solution)/shard_map/scatter-add | solution.py:82
  442.3 40.1 %psum.67 = f32[32,32]{1,0:T(8,128)S(1)} all-reduce(f32[32,32]{1,0:T(8,128)S(1)} %fusion.205), channel_id=1, replica_groups=mesh['seg'=4,'sub'=8] {'seg','sub'}, use_global_device_ids=true, to_apply=%region_11.15 | all-reduce | flops 1024 | bytes 8192 | tf_op jit(solution)/shard_map/psum | solution.py:93
  485.8 8.2 fusion.8
  494.5 41.6 %psum.68 = f32[32,32]{1,0:T(8,128)S(1)} all-reduce(f32[32,32]{1,0:T(8,128)S(1)} %fusion.96), channel_id=1, replica_groups=mesh['seg'=4,'sub'=8] {'seg','sub'}, use_global_device_ids=true, to_apply=%region_12.16 | all-reduce | flops 1024 | bytes 8192 | tf_op jit(solution)/shard_map/psum | solution.py:93
  547.4 10.9 %gather_fusion.5 = f32[3072,32]{1,0:T(8,128)} fusion(f32[32,3072]{0,1:T(8,128)S(1)} %copy.147, s32[3072]{0:T(1024)S(1)} %fusion.141), kind=kCustom, calls=%fused_computation.4.clone | custom fusion | bytes 798720 | tf_op jit(solution)/shard_map/jit(_take)/gather | solution.py:75
  582.5 18.0 %scatter_fusion.4 = f32[32,3072]{0,1:T(8,128)S(1)} fusion(f32[32,3072]{0,1:T(8,128)S(1)} %copy.147, s32[3072]{0:T(1024)S(1)} %bitcast.278, f32[3072,32]{1,0:T(8,128)} %copy.148), kind=kCustom, calls=%fused_computation.13 | custom fusion | flops 98304 | bytes 1191936 | tf_op jit(solution)/shard_map/scatter-add | solution.py:82
  605.3 8.2 fusion.6
  613.7 8.8 fusion.4
  627.4 39.3 %psum.69 = f32[32,72]{1,0:T(8,128)S(1)} all-reduce(f32[32,72]{1,0:T(8,128)S(1)} %fusion.146), channel_id=1, replica_groups=mesh['seg'=4,'sub'=8] {'seg','sub'}, use_global_device_ids=true, to_apply=%region_14.18 | all-reduce | flops 2304 | bytes 18432 | tf_op jit(solution)/shard_map/psum | solution.py:103
  670.8 10.9 %gather_fusion.6 = f32[3072,32]{1,0:T(8,128)} fusion(f32[32,3072]{0,1:T(8,128)S(1)} %copy.153, s32[3072]{0:T(1024)S(1)} %fusion.141), kind=kCustom, calls=%fused_computation.5.clone | custom fusion | bytes 798720 | tf_op jit(solution)/shard_map/jit(_take)/gather | solution.py:75
  706.0 18.2 %scatter_fusion.5 = f32[32,3072]{0,1:T(8,128)S(1)} fusion(f32[32,3072]{0,1:T(8,128)S(1)} %copy.153, s32[3072]{0:T(1024)S(1)} %bitcast.279, f32[3072,32]{1,0:T(8,128)} %copy.154), kind=kCustom, calls=%fused_computation.14 | custom fusion | flops 98304 | bytes 1191936 | tf_op jit(solution)/shard_map/scatter-add | solution.py:82
  729.0 41.7 %psum.70 = f32[32,32]{1,0:T(8,128)S(1)} all-reduce(f32[32,32]{1,0:T(8,128)S(1)} %fusion.207), channel_id=1, replica_groups=mesh['seg'=4,'sub'=8] {'seg','sub'}, use_global_device_ids=true, to_apply=%region_16.20 | all-reduce | flops 1024 | bytes 8192 | tf_op jit(solution)/shard_map/psum | solution.py:93
  772.8 8.1 fusion
  781.5 40.0 %psum.71 = f32[32,32]{1,0:T(8,128)S(1)} all-reduce(f32[32,32]{1,0:T(8,128)S(1)} %fusion.97), channel_id=1, replica_groups=mesh['seg'=4,'sub'=8] {'seg','sub'}, use_global_device_ids=true, to_apply=%region_17.21 | all-reduce | flops 1024 | bytes 8192 | tf_op jit(solution)/shard_map/psum | solution.py:93
  832.7 10.9 %gather_fusion.7 = f32[3072,32]{1,0:T(8,128)} fusion(f32[32,3072]{0,1:T(8,128)S(1)} %copy.163, s32[3072]{0:T(1024)S(1)} %fusion.141), kind=kCustom, calls=%fused_computation.6.clone | custom fusion | bytes 798720 | tf_op jit(solution)/shard_map/jit(_take)/gather | solution.py:75
  865.0 17.5 %scatter_fusion.6 = f32[32,3072]{0,1:T(8,128)S(1)} fusion(f32[32,3072]{0,1:T(8,128)S(1)} %copy.163, s32[3072]{0:T(1024)S(1)} %bitcast.280, f32[3072,32]{1,0:T(8,128)S(1)} %copy.164), kind=kCustom, calls=%fused_computation.15 | custom fusion | flops 98304 | bytes 1191936 | tf_op jit(solution)/shard_map/scatter-add | solution.py:82
  (307 shorter events, 253.3 us)
Async XLA Ops:
  0.6 87.5 %copy-start = (f32[1,1,4,3072]{3,2,1,0:T(4,128)S(1)}, f32[1,1,4,3072]{3,2,1,0:T(4,128)}, u32[]{:S(2)}) copy-start(f32[1,1,4,3072]{3,2,1,0:T(4,128)} %param.18) | copy-start | bytes 147460
  23.7 23.1 %collective-permute-start = (f32[32,1,768]{2,0,1:T(8,128)S(1)}, f32[32,1,768]{2,0,1:T(8,128)S(1)}, u32[]{:S(2)}, u32[]{:S(2)}) collective-permute-start(f32[32,1,768]{2,0,1:T(8,128)S(1)} %get-tuple-element.51), channel_id=1, source_target_pairs={{0,1},{1,2},{2,3},{3,4},{4,5},{5,6},{6,7},{7,0},{8,9},{9,10},{10,1... | collective-permute-start | bytes 294920 | tf_op jit(solution)/shard_map/ppermute | solution.py:21
  26.7 20.1 %collective-permute-start.1 = (f32[32,1,768]{2,0,1:T(8,128)S(1)}, f32[32,1,768]{2,0,1:T(8,128)S(1)}, u32[]{:S(2)}, u32[]{:S(2)}) collective-permute-start(f32[32,1,768]{2,0,1:T(8,128)S(1)} %get-tuple-element.54), channel_id=1, source_target_pairs={{1,0},{2,1},{3,2},{4,3},{5,4},{6,5},{7,6},{0,7},{9,8},{10,9},{11,1... | collective-permute-start | bytes 294920 | tf_op jit(solution)/shard_map/ppermute | solution.py:23
  29.8 17.0 %collective-permute-start.2 = (f32[32,1,768]{2,0,1:T(8,128)S(1)}, f32[32,1,768]{2,0,1:T(8,128)S(1)}, u32[]{:S(2)}, u32[]{:S(2)}) collective-permute-start(f32[32,1,768]{2,0,1:T(8,128)S(1)} %get-tuple-element.53), channel_id=1, source_target_pairs={{0,8},{8,16},{16,24},{1,9},{9,17},{17,25},{2,10},{10,18},{18,26},{... | collective-permute-start | bytes 294920 | tf_op jit(solution)/shard_map/ppermute | solution.py:21
  31.2 15.6 %collective-permute-start.3 = (f32[32,1,768]{2,0,1:T(8,128)S(1)}, f32[32,1,768]{2,0,1:T(8,128)S(1)}, u32[]{:S(2)}, u32[]{:S(2)}) collective-permute-start(f32[32,1,768]{2,0,1:T(8,128)S(1)} %get-tuple-element.52), channel_id=1, source_target_pairs={{8,0},{16,8},{24,16},{9,1},{17,9},{25,17},{10,2},{18,10},{26,18},{... | collective-permute-start | bytes 294920 | tf_op jit(solution)/shard_map/ppermute | solution.py:23
  158.6 7.5 collective-permute-start.4
  160.9 5.7 collective-permute-start.5
  163.3 3.2 collective-permute-start.6
  164.6 5.7 collective-permute-start.7
  277.9 8.1 collective-permute-start.10
  279.2 6.8 collective-permute-start.11
  280.5 7.5 collective-permute-start.8
  282.8 6.2 collective-permute-start.9
  403.2 11.1 %collective-permute-start.12 = (f32[32,1,768]{2,0,1:T(8,128)}, f32[32,1,768]{2,0,1:T(8,128)S(1)}, u32[]{:S(2)}, u32[]{:S(2)}) collective-permute-start(f32[32,1,768]{2,0,1:T(8,128)} %get-tuple-element.39), channel_id=1, source_target_pairs={{0,1},{1,2},{2,3},{3,4},{4,5},{5,6},{6,7},{7,0},{8,9},{9,10},{10,1... | collective-permute-start | bytes 294920 | tf_op jit(solution)/shard_map/ppermute | solution.py:21
  405.5 8.8 collective-permute-start.13
  408.0 6.4 collective-permute-start.14
  409.9 5.2 collective-permute-start.15
  485.7 58.9 %copy-start.3 = (f32[32,3072]{1,0:T(8,128)}, f32[32,3072]{1,0:T(8,128)S(1)}, u32[]{:S(2)}) copy-start(f32[32,3072]{1,0:T(8,128)S(1)} %get-tuple-element.60) | copy-start | bytes 1179652
  485.8 57.5 %copy-start.5 = (f32[32,3072]{1,0:T(8,128)S(1)}, f32[32,3072]{1,0:T(8,128)}, u32[]{:S(2)}) copy-start(f32[32,3072]{1,0:T(8,128)} %convolution_subtract_fusion.2) | copy-start | bytes 1179652
  566.2 11.6 %collective-permute-start.16 = (f32[32,1,768]{2,0,1:T(8,128)}, f32[32,1,768]{2,0,1:T(8,128)S(1)}, u32[]{:S(2)}, u32[]{:S(2)}) collective-permute-start(f32[32,1,768]{2,0,1:T(8,128)} %get-tuple-element.35), channel_id=1, source_target_pairs={{0,1},{1,2},{2,3},{3,4},{4,5},{5,6},{6,7},{7,0},{8,9},{9,10},{10,1... | collective-permute-start | bytes 294920 | tf_op jit(solution)/shard_map/ppermute | solution.py:21
  568.5 9.3 %collective-permute-start.17 = (f32[32,1,768]{2,0,1:T(8,128)}, f32[32,1,768]{2,0,1:T(8,128)}, u32[]{:S(2)}, u32[]{:S(2)}) collective-permute-start(f32[32,1,768]{2,0,1:T(8,128)} %get-tuple-element.38), channel_id=1, source_target_pairs={{1,0},{2,1},{3,2},{4,3},{5,4},{6,5},{7,6},{0,7},{9,8},{10,9},{11,1... | collective-permute-start | bytes 294920 | tf_op jit(solution)/shard_map/ppermute | solution.py:23
  570.9 6.8 collective-permute-start.18
  572.8 5.2 collective-permute-start.19
  689.6 11.0 %collective-permute-start.20 = (f32[32,1,768]{2,0,1:T(8,128)}, f32[32,1,768]{2,0,1:T(8,128)S(1)}, u32[]{:S(2)}, u32[]{:S(2)}) collective-permute-start(f32[32,1,768]{2,0,1:T(8,128)} %get-tuple-element.31), channel_id=1, source_target_pairs={{0,1},{1,2},{2,3},{3,4},{4,5},{5,6},{6,7},{7,0},{8,9},{9,10},{10,1... | collective-permute-start | bytes 294920 | tf_op jit(solution)/shard_map/ppermute | solution.py:21
  691.9 8.8 collective-permute-start.21
  694.4 6.3 collective-permute-start.22
  696.3 5.3 collective-permute-start.23
  772.8 55.8 %copy-start.4 = (f32[32,3072]{1,0:T(8,128)S(1)}, f32[32,3072]{1,0:T(8,128)}, u32[]{:S(2)}) copy-start(f32[32,3072]{1,0:T(8,128)} %convolution_subtract_fusion.1) | copy-start | bytes 1179652
  850.9 10.1 %collective-permute-start.24 = (f32[32,1,768]{2,0,1:T(8,128)S(1)}, f32[32,1,768]{2,0,1:T(8,128)S(1)}, u32[]{:S(2)}, u32[]{:S(2)}) collective-permute-start(f32[32,1,768]{2,0,1:T(8,128)S(1)} %get-tuple-element.27), channel_id=1, source_target_pairs={{0,1},{1,2},{2,3},{3,4},{4,5},{5,6},{6,7},{7,0},{8,9},{9,10},{10,1... | collective-permute-start | bytes 294920 | tf_op jit(solution)/shard_map/ppermute | solution.py:21
  853.2 7.7 collective-permute-start.25
  855.7 5.3 collective-permute-start.26
  857.0 5.7 collective-permute-start.27
  (23 other events, 270.5 us)
where the time goes:
time: 892 us; the launch traced here: 884 us
  blocking collectives  338 us (38%)
  other arithmetic  206 us (23%)
  local copies, waits for them, and re-layouts  142 us (16%)
  matrix products  127 us (14%)
  starting transfers between devices  54.8 us (6%)
  waiting for transfers between devices  11.2 us (1%)
    psum x5, blocking collectives, global_inner(): return lax.psum(local_terms, ('seg', 'sub'))  203 us
    psum x3, blocking collectives, precondition(): lax.psum(jnp.dot(local_coarse, table, precision=HIGH), ('seg', 'sub'))  135 us
    scatter-add x7, other arithmetic, assemble(): return values.at[:, slot_rows].add(received.reshape(block, width))  125 us
    dot_general x12, matrix products, local_product(): both = jnp.dot(stacked, matrix, preferred_element_type=jnp.float32)  87.7 us
    gather x7, local copies, waits for them, and re-layouts, assemble(): jnp.take(values, slot_rows, axis=1).reshape(block, 4, face_width)  76.2 us
    ppermute x14, starting transfers between devices, with_halo(): lax.ppermute(tail, axis, [(i, (i + 1) % count) for i in range(ends)])  27.8 us
    ppermute x14, starting transfers between devices, with_halo(): lax.ppermute(head, axis, [((i + 1) % count, i) for i in range(ends)])  27 us
    select_n x7, other arithmetic, assemble(): jnp.take(values, slot_rows, axis=1).reshape(block, 4, face_width)  23.4 us
  transfers between devices with their start and end apart: 28, of which 9 were waited for; matrix products, arithmetic and copies ran while one was open for 3% of the time, Pallas kernels for 0%

commit v1 on v0

--- a/solution.py
+++ b/solution.py
@@ -1,6 +1,10 @@
+import functools
+
 import jax
 import jax.numpy as jnp
 from jax import lax
+from jax.experimental import pallas as pl
+from jax.experimental.pallas import tpu as pltpu
 from jax.sharding import PartitionSpec as P
 
 DEG = 3
@@ -10,21 +14,126 @@
 HIGH = lax.Precision.HIGHEST
 
 
-def with_halo(cells, sides, width, closed):
-    for axis, dim in sides:
-        count = lax.axis_size(axis)
-        ends = count if closed else count - 1
-        head = lax.slice_in_dim(cells, 0, width, axis=dim)
-        tail = lax.slice_in_dim(cells, cells.shape[dim] - width, cells.shape[dim], axis=dim)
-        cells = jnp.concatenate(
-            [
-                lax.ppermute(tail, axis, [(i, (i + 1) % count) for i in range(ends)]),
-                cells,
-                lax.ppermute(head, axis, [((i + 1) % count, i) for i in range(ends)]),
-            ],
-            axis=dim,
+MESH = pl.DeviceIdType.MESH
+LANES = 128
+
+
+def greet(peers):
+    barrier = pltpu.get_barrier_semaphore()
+    for peer in peers:
+        pl.semaphore_signal(barrier, inc=1, device_id=peer, device_id_type=MESH)
+    pl.semaphore_wait(barrier, len(peers))
+
+
+def total_kernel(counts, x_ref, o_ref, first, second, first_sems, second_sems):
+    stages = (("sub", first, first_sems), ("seg", second, second_sems))
+    places = {axis: lax.axis_index(axis) for axis in counts}
+
+    def peer(axis, shift):
+        return lax.rem(places[axis] + (shift + counts[axis]) % counts[axis], counts[axis])
+
+    greet([{axis: peer(axis, d)} for axis, _, _ in stages for d in range(1, counts[axis])])
+    value = x_ref[...]
+    for stage, (axis, held, sems) in enumerate(stages):
+        own = held.at[places[axis]]
+        source = x_ref if stage == 0 else own
+        held[places[axis]] = value
+        sends = []
+        for d in range(1, counts[axis]):
+            send = pltpu.make_async_remote_copy(
+                src_ref=source,
+                dst_ref=own,
+                send_sem=sems.at[0, d],
+                recv_sem=sems.at[1, d],
+                device_id={axis: peer(axis, d)},
+                device_id_type=MESH,
+            )
+            send.start()
+            sends.append(send)
+        for d in range(1, counts[axis]):
+            pltpu.make_async_remote_copy(
+                src_ref=source,
+                dst_ref=held.at[peer(axis, -d)],
+                send_sem=sems.at[0, d],
+                recv_sem=sems.at[1, d],
+                device_id={axis: peer(axis, d)},
+                device_id_type=MESH,
+            ).wait_recv()
+        for send in sends:
+            send.wait_send()
+        value = held[0]
+        for i in range(1, counts[axis]):
+            value = value + held[i]
+    o_ref[...] = value
+
+
+def global_sum(terms, collective_id):
+    rows, columns = terms.shape
+    padded = -(-columns // LANES) * LANES
+    counts = {"sub": lax.axis_size("sub"), "seg": lax.axis_size("seg")}
+    shape = (rows, padded)
+    summed = pl.pallas_call(
+        functools.partial(total_kernel, counts),
+        out_shape=jax.ShapeDtypeStruct(shape, jnp.float32),
+        in_specs=[pl.BlockSpec(memory_space=pltpu.VMEM)],
+        out_specs=pl.BlockSpec(memory_space=pltpu.VMEM),
+        scratch_shapes=[
+            pltpu.VMEM((counts["sub"],) + shape, jnp.float32),
+            pltpu.VMEM((counts["seg"],) + shape, jnp.float32),
+            pltpu.SemaphoreType.DMA((2, counts["sub"])),
+            pltpu.SemaphoreType.DMA((2, counts["seg"])),
+        ],
+        compiler_params=pltpu.CompilerParams(
+            collective_id=collective_id, has_side_effects=True
+        ),
+    )(jnp.pad(terms, ((0, 0), (0, padded - columns))))
+    return summed[:, :columns]
+
+
+def halo_kernel(counts, slots_ref, mask_ref, o_ref, held, sems):
+    width = slots_ref.shape[1] // 4
+
+    def peer(axis, shift):
+        count = counts[axis]
+        return {axis: lax.rem(lax.axis_index(axis) + (shift + count) % count, count)}
+
+    routes = (
+        (1, 0, peer("sub", 1)),
+        (0, 1, peer("sub", -1)),
+        (3, 2, peer("seg", 1)),
+        (2, 3, peer("seg", -1)),
+    )
+    greet([target for _, _, target in routes])
+    copies = []
+    for face, landing, target in routes:
+        copy = pltpu.make_async_remote_copy(
+            src_ref=slots_ref.at[:, pl.ds(face * width, width)],
+            dst_ref=held.at[:, pl.ds(landing * width, width)],
+            send_sem=sems.at[0, landing],
+            recv_sem=sems.at[1, landing],
+            device_id=target,
+            device_id_type=MESH,
         )
-    return cells
+        copy.start()
+        copies.append(copy)
+    for copy in copies:
+        copy.wait()
+    o_ref[...] = held[...] * mask_ref[...]
+
+
+def exchange(slots, mask):
+    counts = {"sub": lax.axis_size("sub"), "seg": lax.axis_size("seg")}
+    return pl.pallas_call(
+        functools.partial(halo_kernel, counts),
+        out_shape=jax.ShapeDtypeStruct(slots.shape, jnp.float32),
+        in_specs=[pl.BlockSpec(memory_space=pltpu.VMEM)] * 2,
+        out_specs=pl.BlockSpec(memory_space=pltpu.VMEM),
+        scratch_shapes=[
+            pltpu.VMEM(slots.shape, jnp.float32),
+            pltpu.SemaphoreType.DMA((2, 4)),
+        ],
+        compiler_params=pltpu.CompilerParams(collective_id=2, has_side_effects=True),
+    )(slots, mask)
 
 
 def symmetric(matrix):
@@ -65,32 +174,41 @@
     live_mask = (jnp.arange(face_width, dtype=jnp.int32)[None, :] < lengths[:, None]).astype(
         jnp.float32
     )
-    live_weight = (
-        jnp.zeros((width,), jnp.float32).at[slot_rows].set(1.0 - 0.5 * live_mask.reshape(-1))
-    )
+    mask_row = live_mask.reshape(1, width)
+    placing = lax.optimization_barrier(
+        (slot_rows[:, None] == jnp.arange(width, dtype=jnp.int32)[None, :]).astype(jnp.bfloat16)
+    )
+    covered = jnp.dot(
+        jnp.broadcast_to(mask_row.astype(jnp.bfloat16), (16, width)),
+        placing,
+        preferred_element_type=jnp.float32,
+    )
+    live_weight = 1.0 - 0.5 * covered[0]
     my_faces = primal_index[seg_at, sub_at]
     coarse_columns = jnp.take(coarse_inverse, my_faces, axis=1)
 
-    def assemble(values):
-        slots = jnp.take(values, slot_rows, axis=1).reshape(block, 4, face_width) * live_mask[None]
-        across = with_halo(slots[:, 0:2], (("sub", 1),), 1, True)
-        along = with_halo(slots[:, 2:4], (("seg", 1),), 1, False)
-        received = (
-            jnp.stack([across[:, 0], across[:, 3], along[:, 0], along[:, 3]], axis=1)
-            * live_mask[None]
-        )
-        return values.at[:, slot_rows].add(received.reshape(block, width))
-
-    def local_product(values):
+    def split_dot(values, right, contract):
         upper = values.astype(jnp.bfloat16)
         upper_back = lax.optimization_barrier(upper).astype(jnp.float32)
         lower = (values - upper_back).astype(jnp.bfloat16)
         stacked = jnp.concatenate([upper, lower], axis=0)
-        both = jnp.dot(stacked, matrix, preferred_element_type=jnp.float32)
+        both = lax.dot_general(
+            stacked,
+            right,
+            (((1,), (contract,)), ((), ())),
+            preferred_element_type=jnp.float32,
+        )
         return both[:block] + both[block:]
 
+    def assemble(values):
+        slots = split_dot(values, placing, 1)
+        return values + split_dot(exchange(slots, mask_row), placing, 0)
+
+    def local_product(values):
+        return split_dot(values, matrix, 0)
+
     def global_inner(local_terms):
-        return lax.psum(local_terms, ("seg", "sub"))
+        return global_sum(local_terms, 0)
 
     def precondition(weighted):
         solve = relax * weighted
@@ -100,7 +218,7 @@
         table = (my_faces[:, None] == jnp.arange(coarse_count, dtype=jnp.int32)[None, :]).astype(
             jnp.float32
         )
-        coarse_sum = lax.psum(jnp.dot(local_coarse, table, precision=HIGH), ("seg", "sub"))
+        coarse_sum = global_sum(jnp.dot(local_coarse, table, precision=HIGH), 1)
         picked = jnp.dot(coarse_sum, coarse_columns, precision=HIGH)
         correction = jnp.dot(picked, basis, precision=HIGH)
         return assemble((solve + correction) * live_weight[None, :])

time: 892 us -> 509 us (0.57)
  blocking collectives: 338 us -> 0 us
  Pallas kernels: 0 us -> 173 us
  other arithmetic: 206 us -> 70.6 us
  local copies, waits for them, and re-layouts: 142 us -> 21.9 us
  matrix products: 127 us -> 230 us
  starting transfers between devices: 54.8 us -> 0 us
  waiting for transfers between devices: 11.2 us -> 0 us
    psum x8 -> x0, blocking collectives: 338 us -> none  [the longest x5 203 us: global_inner(): return lax.psum(local_terms, ('seg', 'sub'))]
    pallas_call x0 -> x16, Pallas kernels: none -> 173 us  [the longest x9 101 us: global_sum(): pl.pallas_call(functools.partial(total_kernel, counts), out_shape=jax.Sha...]
    dot_general x15 -> x30, matrix products: 88.4 us -> 214 us  [the longest x26 211 us: split_dot(): lax.dot_general(stacked, right, (((1,), (contract,)), ((), ())), preferre...]
    scatter-add x7 -> x0, other arithmetic: 125 us -> none  [assemble(): return values.at[:, slot_rows].add(received.reshape(block, width))]
    gather x7 -> x0, local copies, waits for them, and re-layouts: 76.2 us -> none  [assemble(): jnp.take(values, slot_rows, axis=1).reshape(block, 4, face_width)]
    ppermute x28 -> x0, starting transfers between devices: 54.8 us -> none  [the longest x14 27.8 us: with_halo(): lax.ppermute(tail, axis, [(i, (i + 1) % count) for i in range(ends)])]
    select_n x8 -> x0, other arithmetic: 23.4 us -> none  [the longest x7 23.4 us: assemble(): jnp.take(values, slot_rows, axis=1).reshape(block, 4, face_width)]
    convert_element_type x24 -> x45, other arithmetic: 5.67 us -> 25.7 us  [the longest x26 9.11 us: split_dot(): lower = (values - upper_back).astype(jnp.bfloat16)]
  transfers between devices with their start and end apart: 28 -> 0, of which waited for: 9 -> 0; matrix products, arithmetic and copies ran while one was open for 3% -> 0% of each run, Pallas kernels for 0% -> 0%
where the time goes in v1:
time: 509 us; the launch traced here: 500 us
  matrix products  230 us (45%)
  Pallas kernels  173 us (34%)
  other arithmetic  70.6 us (14%)
  local copies, waits for them, and re-layouts  21.9 us (4%)
    dot_general x26, matrix products, split_dot(): lax.dot_general(stacked, right, (((1,), (contract,)), ((), ())), preferre...  211 us
    pallas_call x9, Pallas kernels, global_sum(): pl.pallas_call(functools.partial(total_kernel, counts), out_shape=jax.Sha...  101 us
    pallas_call x7, Pallas kernels, exchange(): pl.pallas_call(functools.partial(halo_kernel, counts), out_shape=jax.Shap...  72 us
    another operation x9, other arithmetic, body(): factor = jnp.linalg.cholesky(curvature)  10.8 us

profile of v1, /device:TPU:0, one launch (start us, length us, event | category | flops | bytes accessed | tf_op | source)
XLA Modules:
  0.0 499.5 jit_solution(13327467817878991981)
XLA Ops:
  27.1 9.7 %fusion.59 = f32[64,3072]{1,0:T(8,128)S(1)} fusion(bf16[3072,3072]{1,0:T(8,128)(2,1)} %copy-done.1, bf16[32,3072]{1,0:T(8,128)(2,1)S(1)} %fusion.153, bf16[32,3072]{1,0:T(8,128)(2,1)S(1)} %bitcast_convert_fusion), kind=kOutput, calls=%fused_computation.98 | convolution fusion | flops 1208745984 | bytes 20054016 | tf_op jit(solution)/shard_map/dot_general | solution.py:195
  37.5 12.4 %shard_map.95 = f32[32,3072]{1,0:T(8,128)} custom-call(f32[32,3072]{1,0:T(8,128)} %slice_add_fusion.25.slots_ref, f32[1,3072]{1,0:T(1,128)} %bitcast.239), custom_call_target="tpu_custom_call" | custom-call | tf_op jit(solution)/shard_map/pallas_call | solution.py:126
  61.5 10.5 %shard_map.96 = f32[32,128]{1,0:T(8,128)} custom-call(f32[32,128]{1,0:T(8,128)} %pad.29.x_ref), custom_call_target="tpu_custom_call" | custom-call | tf_op jit(solution)/shard_map/pallas_call | solution.py:75
  73.0 8.2 %fusion.23 = f32[64,3072]{1,0:T(8,128)S(1)} fusion(bf16[1,1,3072,3072]{3,2,1,0:T(8,128)(2,1)} %param.12, bf16[32,3072]{1,0:T(8,128)(2,1)S(1)} %subtract_convert_fusion.23, bf16[32,3072]{1,0:T(8,128)(2,1)S(1)} %get-tuple-element.22), kind=kOutput, calls=%fused_computation.25 | convolution fusion | flops 1208745984 | bytes 20054016 | tf_op jit(solution)/shard_map/dot_general | solution.py:195
  81.5 8.9 %fusion.21 = f32[64,3072]{1,0:T(8,128)S(1)} fusion(bf16[1,1,3072,3072]{3,2,1,0:T(8,128)(2,1)} %param.12, bf16[32,3072]{1,0:T(8,128)(2,1)S(1)} %subtract_convert_fusion.22, bf16[32,3072]{1,0:T(8,128)(2,1)S(1)} %get-tuple-element.20), kind=kOutput, calls=%fused_computation.23 | convolution fusion | flops 1208745984 | bytes 20054016 | tf_op jit(solution)/shard_map/dot_general | solution.py:195
  94.6 9.7 %fusion.76 = f32[64,3072]{1,0:T(8,128)S(1)} fusion(bf16[3072,3072]{1,0:T(8,128)(2,1)} %copy-done.1, bf16[32,3072]{1,0:T(8,128)(2,1)S(1)} %subtract_convert_fusion.20, bf16[32,3072]{1,0:T(8,128)(2,1)S(1)} %get-tuple-element.30), kind=kOutput, calls=%fused_computation.115 | convolution fusion | flops 1208745984 | bytes 20054016 | tf_op jit(solution)/shard_map/dot_general | solution.py:195
  105.1 9.9 %shard_map.97 = f32[32,3072]{1,0:T(8,128)} custom-call(f32[32,3072]{1,0:T(8,128)} %slice_add_fusion.20.slots_ref, f32[1,3072]{1,0:T(1,128)} %bitcast.240), custom_call_target="tpu_custom_call" | custom-call | tf_op jit(solution)/shard_map/pallas_call | solution.py:126
  126.4 11.2 %shard_map.99 = f32[32,128]{1,0:T(8,128)} custom-call(f32[32,128]{1,0:T(8,128)} %pad.31.x_ref), custom_call_target="tpu_custom_call" | custom-call | tf_op jit(solution)/shard_map/pallas_call | solution.py:75
  155.1 11.9 %shard_map.98 = f32[32,128]{1,0:T(8,128)} custom-call(f32[32,128]{1,0:T(8,128)} %pad.30.x_ref), custom_call_target="tpu_custom_call" | custom-call | tf_op jit(solution)/shard_map/pallas_call | solution.py:75
  176.9 10.1 %fusion.87 = f32[64,3072]{1,0:T(8,128)S(1)} fusion(bf16[3072,3072]{1,0:T(8,128)(2,1)} %copy-done.1, bf16[32,3072]{1,0:T(8,128)(2,1)S(1)} %subtract_convert_fusion.17, bf16[32,3072]{1,0:T(8,128)(2,1)S(1)} %get-tuple-element.32), kind=kOutput, calls=%fused_computation.126 | convolution fusion | flops 1208745984 | bytes 20054016 | tf_op jit(solution)/shard_map/dot_general | solution.py:195
  187.7 9.6 %shard_map.100 = f32[32,3072]{1,0:T(8,128)} custom-call(f32[32,3072]{1,0:T(8,128)} %slice_add_fusion.17.slots_ref, f32[1,3072]{1,0:T(1,128)} %bitcast.241), custom_call_target="tpu_custom_call" | custom-call | tf_op jit(solution)/shard_map/pallas_call | solution.py:126
  208.9 11.2 %shard_map.101 = f32[32,128]{1,0:T(8,128)} custom-call(f32[32,128]{1,0:T(8,128)} %pad.32.x_ref), custom_call_target="tpu_custom_call" | custom-call | tf_op jit(solution)/shard_map/pallas_call | solution.py:75
  221.1 8.2 %fusion.15 = f32[64,3072]{1,0:T(8,128)S(1)} fusion(bf16[1,1,3072,3072]{3,2,1,0:T(8,128)(2,1)} %param.12, bf16[32,3072]{1,0:T(8,128)(2,1)S(1)} %subtract_convert_fusion.15, bf16[32,3072]{1,0:T(8,128)(2,1)S(1)} %get-tuple-element.14), kind=kOutput, calls=%fused_computation.17 | convolution fusion | flops 1208745984 | bytes 20054016 | tf_op jit(solution)/shard_map/dot_general | solution.py:195
  229.5 8.7 %fusion.13 = f32[64,3072]{1,0:T(8,128)S(1)} fusion(bf16[1,1,3072,3072]{3,2,1,0:T(8,128)(2,1)} %param.12, bf16[32,3072]{1,0:T(8,128)(2,1)S(1)} %subtract_convert_fusion.14, bf16[32,3072]{1,0:T(8,128)(2,1)S(1)} %get-tuple-element.12), kind=kOutput, calls=%fused_computation.15 | convolution fusion | flops 1208745984 | bytes 20054016 | tf_op jit(solution)/shard_map/dot_general | solution.py:195
  242.5 9.8 %fusion.104 = f32[64,3072]{1,0:T(8,128)S(1)} fusion(bf16[3072,3072]{1,0:T(8,128)(2,1)} %copy-done.1, bf16[32,3072]{1,0:T(8,128)(2,1)S(1)} %subtract_convert_fusion.12, bf16[32,3072]{1,0:T(8,128)(2,1)S(1)} %get-tuple-element.34), kind=kOutput, calls=%fused_computation.143 | convolution fusion | flops 1208745984 | bytes 20054016 | tf_op jit(solution)/shard_map/dot_general | solution.py:195
  253.1 10.1 %shard_map.102 = f32[32,3072]{1,0:T(8,128)} custom-call(f32[32,3072]{1,0:T(8,128)} %slice_add_fusion.12.slots_ref, f32[1,3072]{1,0:T(1,128)} %bitcast.242), custom_call_target="tpu_custom_call" | custom-call | tf_op jit(solution)/shard_map/pallas_call | solution.py:126
  265.3 8.1 %fusion.108 = f32[64,3072]{1,0:T(8,128)S(1)} fusion(bf16[3072,3072]{1,0:T(8,128)(2,1)} %copy-done.1, bf16[32,3072]{1,0:T(8,128)(2,1)S(1)} %subtract_convert_fusion.11, bf16[32,3072]{1,0:T(8,128)(2,1)S(1)} %convert_element_type.330), kind=kOutput, calls=%fused_computation.147 | convolution fusion | flops 1208745984 | bytes 20054016 | tf_op jit(solution)/shard_map/dot_general | solution.py:195
  274.4 10.7 %shard_map.103 = f32[32,128]{1,0:T(8,128)} custom-call(f32[32,128]{1,0:T(8,128)} %pad.33.x_ref), custom_call_target="tpu_custom_call" | custom-call | tf_op jit(solution)/shard_map/pallas_call | solution.py:75
  294.4 8.1 %fusion.9 = f32[64,3072]{1,0:T(8,128)S(1)} fusion(bf16[1,1,3072,3072]{3,2,1,0:T(8,128)(2,1)} %param.12, bf16[32,3072]{1,0:T(8,128)(2,1)S(1)} %subtract_convert_fusion.10, bf16[32,3072]{1,0:T(8,128)(2,1)S(1)} %get-tuple-element.36), kind=kOutput, calls=%fused_computation.11 | convolution fusion | flops 1208745984 | bytes 20054016 | tf_op jit(solution)/shard_map/dot_general | solution.py:195
  303.6 11.8 %shard_map.104 = f32[32,128]{1,0:T(8,128)} custom-call(f32[32,128]{1,0:T(8,128)} %pad.34.x_ref), custom_call_target="tpu_custom_call" | custom-call | tf_op jit(solution)/shard_map/pallas_call | solution.py:75
  325.2 9.7 %fusion.115 = f32[64,3072]{1,0:T(8,128)S(1)} fusion(bf16[3072,3072]{1,0:T(8,128)(2,1)} %copy-done.1, bf16[32,3072]{1,0:T(8,128)(2,1)S(1)} %subtract_convert_fusion.9, bf16[32,3072]{1,0:T(8,128)(2,1)S(1)} %get-tuple-element.38), kind=kOutput, calls=%fused_computation.154 | convolution fusion | flops 1208745984 | bytes 20054016 | tf_op jit(solution)/shard_map/dot_general | solution.py:195
  335.7 10.3 %shard_map.105 = f32[32,3072]{1,0:T(8,128)} custom-call(f32[32,3072]{1,0:T(8,128)} %slice_add_fusion.9.slots_ref, f32[1,3072]{1,0:T(1,128)} %bitcast.243), custom_call_target="tpu_custom_call" | custom-call | tf_op jit(solution)/shard_map/pallas_call | solution.py:126
  357.5 10.7 %shard_map.106 = f32[32,128]{1,0:T(8,128)} custom-call(f32[32,128]{1,0:T(8,128)} %pad.35.x_ref), custom_call_target="tpu_custom_call" | custom-call | tf_op jit(solution)/shard_map/pallas_call | solution.py:75
  369.2 8.5 %fusion.7 = f32[64,3072]{1,0:T(8,128)S(1)} fusion(bf16[1,1,3072,3072]{3,2,1,0:T(8,128)(2,1)} %param.12, bf16[32,3072]{1,0:T(8,128)(2,1)S(1)} %subtract_convert_fusion.7, bf16[32,3072]{1,0:T(8,128)(2,1)S(1)} %get-tuple-element.8), kind=kOutput, calls=%fused_computation.9 | convolution fusion | flops 1208745984 | bytes 20054016 | tf_op jit(solution)/shard_map/dot_general | solution.py:195
  377.8 8.5 %fusion.5 = f32[64,3072]{1,0:T(8,128)S(1)} fusion(bf16[1,1,3072,3072]{3,2,1,0:T(8,128)(2,1)} %param.12, bf16[32,3072]{1,0:T(8,128)(2,1)S(1)} %subtract_convert_fusion.6, bf16[32,3072]{1,0:T(8,128)(2,1)S(1)} %get-tuple-element.6), kind=kOutput, calls=%fused_computation.7 | convolution fusion | flops 1208745984 | bytes 20054016 | tf_op jit(solution)/shard_map/dot_general | solution.py:195
  390.6 9.7 %fusion.132 = f32[64,3072]{1,0:T(8,128)S(1)} fusion(bf16[3072,3072]{1,0:T(8,128)(2,1)} %copy-done.1, bf16[32,3072]{1,0:T(8,128)(2,1)S(1)} %subtract_convert_fusion.4, bf16[32,3072]{1,0:T(8,128)(2,1)S(1)} %get-tuple-element.40), kind=kOutput, calls=%fused_computation.171 | convolution fusion | flops 1208745984 | bytes 20054016 | tf_op jit(solution)/shard_map/dot_general | solution.py:195
  401.0 10.0 %shard_map.107 = f32[32,3072]{1,0:T(8,128)} custom-call(f32[32,3072]{1,0:T(8,128)} %slice_add_fusion.4.slots_ref, f32[1,3072]{1,0:T(1,128)} %bitcast.244), custom_call_target="tpu_custom_call" | custom-call | tf_op jit(solution)/shard_map/pallas_call | solution.py:126
  422.3 11.2 %shard_map.108 = f32[32,128]{1,0:T(8,128)} custom-call(f32[32,128]{1,0:T(8,128)} %pad.36.x_ref), custom_call_target="tpu_custom_call" | custom-call | tf_op jit(solution)/shard_map/pallas_call | solution.py:75
  436.0 8.4 %fusion.1 = f32[64,3072]{1,0:T(8,128)S(1)} fusion(bf16[1,1,3072,3072]{3,2,1,0:T(8,128)(2,1)} %param.12, bf16[32,3072]{1,0:T(8,128)(2,1)S(1)} %subtract_convert_fusion.2, bf16[32,3072]{1,0:T(8,128)(2,1)S(1)} %get-tuple-element.42), kind=kOutput, calls=%fused_computation.3 | convolution fusion | flops 1208745984 | bytes 20054016 | tf_op jit(solution)/shard_map/dot_general | solution.py:195
  445.5 11.9 %shard_map.109 = f32[32,128]{1,0:T(8,128)} custom-call(f32[32,128]{1,0:T(8,128)} %pad.37.x_ref), custom_call_target="tpu_custom_call" | custom-call | tf_op jit(solution)/shard_map/pallas_call | solution.py:75
  468.0 9.7 %fusion.143 = f32[64,3072]{1,0:T(8,128)S(1)} fusion(bf16[3072,3072]{1,0:T(8,128)(2,1)} %copy-done.1, bf16[32,3072]{1,0:T(8,128)(2,1)S(1)} %subtract_convert_fusion.1, bf16[32,3072]{1,0:T(8,128)(2,1)S(1)} %get-tuple-element.44), kind=kOutput, calls=%fused_computation.182 | convolution fusion | flops 1208745984 | bytes 20054016 | tf_op jit(solution)/shard_map/dot_general | solution.py:195
  478.4 9.6 %shard_map.110 = f32[32,3072]{1,0:T(8,128)} custom-call(f32[32,3072]{1,0:T(8,128)} %slice_add_fusion.1.slots_ref, f32[1,3072]{1,0:T(1,128)} %bitcast.245), custom_call_target="tpu_custom_call" | custom-call | tf_op jit(solution)/shard_map/pallas_call | solution.py:126
  (207 shorter events, 178.5 us)
Async XLA Ops:
  0.6 59.6 %copy-start = (f32[1,1,4,3072]{3,2,1,0:T(4,128)S(1)}, f32[1,1,4,3072]{3,2,1,0:T(4,128)}, u32[]{:S(2)}) copy-start(f32[1,1,4,3072]{3,2,1,0:T(4,128)} %param.16) | copy-start | bytes 147460
  18.1 6.5 %copy-start.1 = (bf16[3072,3072]{1,0:T(8,128)(2,1)}, bf16[3072,3072]{1,0:T(8,128)(2,1)S(1)}, u32[]{:S(2)}) copy-start(bf16[3072,3072]{1,0:T(8,128)(2,1)S(1)} %fusion) | copy-start | bytes 56623108
  36.7 23.4 %copy-start.2 = (f32[1,1,32,3072]{3,2,1,0:T(8,128)S(1)}, f32[1,1,32,3072]{3,2,1,0:T(8,128)}, u32[]{:S(2)}) copy-start(f32[1,1,32,3072]{3,2,1,0:T(8,128)} %param.11) | copy-start | bytes 1179652
  73.0 17.5 %slice-start = ((s8[18874368]{0:T(1024)(128)(4,1)}), s8[4194304]{0:T(1024)(128)(4,1)S(1)}, s32[]{:S(2)}) async-start(s8[18874368]{0:T(1024)(128)(4,1)} %bitcast.233), calls=%async_computation | async-start | bytes 8388608
  73.0 17.5 %slice-start.1 = ((s8[18874368]{0:T(1024)(128)(4,1)}), s8[4194304]{0:T(1024)(128)(4,1)S(1)}, s32[]{:S(2)}) async-start(s8[18874368]{0:T(1024)(128)(4,1)} %bitcast.233), calls=%async_computation.1 | async-start | bytes 8388608
  73.0 17.5 %slice-start.2 = ((s8[18874368]{0:T(1024)(128)(4,1)}), s8[4194304]{0:T(1024)(128)(4,1)S(1)}, s32[]{:S(2)}) async-start(s8[18874368]{0:T(1024)(128)(4,1)} %bitcast.233), calls=%async_computation.2 | async-start | bytes 8388608
  81.4 9.1 %slice-start.3 = ((s8[18874368]{0:T(1024)(128)(4,1)}), s8[4194304]{0:T(1024)(128)(4,1)S(1)}, s32[]{:S(2)}) async-start(s8[18874368]{0:T(1024)(128)(4,1)} %bitcast.233), calls=%async_computation.3 | async-start | bytes 8388608
  81.5 9.1 %slice-start.4 = ((s8[18874368]{0:T(1024)(128)(4,1)}), s8[2097152]{0:T(1024)(128)(4,1)S(1)}, s32[]{:S(2)}) async-start(s8[18874368]{0:T(1024)(128)(4,1)} %bitcast.233), calls=%async_computation.4 | async-start | bytes 4194304
  221.1 17.3 %slice-start.5 = ((s8[18874368]{0:T(1024)(128)(4,1)}), s8[4194304]{0:T(1024)(128)(4,1)S(1)}, s32[]{:S(2)}) async-start(s8[18874368]{0:T(1024)(128)(4,1)} %bitcast.235), calls=%async_computation.5 | async-start | bytes 8388608
  221.1 17.3 %slice-start.6 = ((s8[18874368]{0:T(1024)(128)(4,1)}), s8[4194304]{0:T(1024)(128)(4,1)S(1)}, s32[]{:S(2)}) async-start(s8[18874368]{0:T(1024)(128)(4,1)} %bitcast.235), calls=%async_computation.6 | async-start | bytes 8388608
  221.1 17.3 %slice-start.7 = ((s8[18874368]{0:T(1024)(128)(4,1)}), s8[4194304]{0:T(1024)(128)(4,1)S(1)}, s32[]{:S(2)}) async-start(s8[18874368]{0:T(1024)(128)(4,1)} %bitcast.235), calls=%async_computation.7 | async-start | bytes 8388608
  229.5 8.9 %slice-start.8 = ((s8[18874368]{0:T(1024)(128)(4,1)}), s8[4194304]{0:T(1024)(128)(4,1)S(1)}, s32[]{:S(2)}) async-start(s8[18874368]{0:T(1024)(128)(4,1)} %bitcast.235), calls=%async_computation.8 | async-start | bytes 8388608
  229.5 9.0 %slice-start.9 = ((s8[18874368]{0:T(1024)(128)(4,1)}), s8[2097152]{0:T(1024)(128)(4,1)S(1)}, s32[]{:S(2)}) async-start(s8[18874368]{0:T(1024)(128)(4,1)} %bitcast.235), calls=%async_computation.9 | async-start | bytes 4194304
  369.1 17.3 %slice-start.10 = ((s8[18874368]{0:T(1024)(128)(4,1)}), s8[4194304]{0:T(1024)(128)(4,1)S(1)}, s32[]{:S(2)}) async-start(s8[18874368]{0:T(1024)(128)(4,1)} %bitcast.237), calls=%async_computation.10 | async-start | bytes 8388608
  369.2 17.3 %slice-start.11 = ((s8[18874368]{0:T(1024)(128)(4,1)}), s8[4194304]{0:T(1024)(128)(4,1)S(1)}, s32[]{:S(2)}) async-start(s8[18874368]{0:T(1024)(128)(4,1)} %bitcast.237), calls=%async_computation.11 | async-start | bytes 8388608
  369.2 17.3 %slice-start.12 = ((s8[18874368]{0:T(1024)(128)(4,1)}), s8[4194304]{0:T(1024)(128)(4,1)S(1)}, s32[]{:S(2)}) async-start(s8[18874368]{0:T(1024)(128)(4,1)} %bitcast.237), calls=%async_computation.12 | async-start | bytes 8388608
  377.8 8.7 %slice-start.13 = ((s8[18874368]{0:T(1024)(128)(4,1)}), s8[4194304]{0:T(1024)(128)(4,1)S(1)}, s32[]{:S(2)}) async-start(s8[18874368]{0:T(1024)(128)(4,1)} %bitcast.237), calls=%async_computation.13 | async-start | bytes 8388608
  377.8 8.8 %slice-start.14 = ((s8[18874368]{0:T(1024)(128)(4,1)}), s8[2097152]{0:T(1024)(128)(4,1)S(1)}, s32[]{:S(2)}) async-start(s8[18874368]{0:T(1024)(128)(4,1)} %bitcast.237), calls=%async_computation.14 | async-start | bytes 4194304
  433.5 32.2 %copy-start.3 = (f32[32,128]{1,0:T(8,128)S(1)}, f32[32,128]{1,0:T(8,128)}, u32[]{:S(2)}) copy-start(f32[32,128]{1,0:T(8,128)} %shard_map.108) | copy-start | bytes 49156
